TPU v7x, 32 devices: a whole 2x2x4 slice. The times are simulated.
32 devices in a mesh: tp: 2 (over x), sp: 16 (over z, y, core).
Axes of the slice: x: 2, y: 2, z: 4, core: 2. Of those that a mesh axis runs over, the one named last changes fastest.
Arguments:
- tokens: bfloat16 [2048, 2048], P('sp'), may hold values from -6 to 6
- item_lengths: int32 [4], replicated, may hold values from 128 to 1536, as said below
- first_gain: bfloat16 [2048], replicated, may hold values from 0.25 to 1.75
- query_weight: bfloat16 [2048, 2048], P('tp'), may hold values from -0.125 to 0.125
- key_weight: bfloat16 [1024, 2048], P('tp'), may hold values from -0.125 to 0.125
- value_weight: bfloat16 [1024, 2048], P('tp'), may hold values from -0.125 to 0.125
- headgate_weight: bfloat16 [16, 2048], P('tp'), may hold values from -0.125 to 0.125
- merge_weight: bfloat16 [2048, 2048], P(None, 'tp'), may hold values from -1 to 1
- query_norm: bfloat16 [128], replicated, may hold values from 0.8984375 to 2
- key_norm: bfloat16 [128], replicated, may hold values from 0.8984375 to 2
- second_gain: bfloat16 [2048], replicated, may hold values from 0.25 to 1.75
- gate_weight: bfloat16 [6144, 2048], P(('tp', 'sp')), may hold values from -0.125 to 0.125
- up_weight: bfloat16 [6144, 2048], P(('tp', 'sp')), may hold values from -0.125 to 0.125
- down_weight: bfloat16 [6144, 2048], P(('tp', 'sp')), may hold values from -0.078125 to 0.078125
- out_cotangent: bfloat16 [2048, 2048], P('sp')
Outputs:
- layer_output: bfloat16 [2048, 2048], P('sp')
- input_grad: float32 [2048, 2048], P('sp')
- first_grad: float32 [2048], replicated
- query_grad: float32 [2048, 2048], P('tp')
- key_grad: float32 [1024, 2048], P('tp')
- value_grad: float32 [1024, 2048], P('tp')
- headgate_grad: float32 [16, 2048], P('tp')
- merge_grad: float32 [2048, 2048], P(None, 'tp')
- query_norm_grad: float32 [128], replicated
- key_norm_grad: float32 [128], replicated
- second_grad: float32 [2048], replicated
- gate_grad: float32 [6144, 2048], P(('tp', 'sp'))
- up_grad: float32 [6144, 2048], P(('tp', 'sp'))
- down_grad: float32 [6144, 2048], P(('tp', 'sp'))
Inputs may be any that keep to these rules, and one draw needn't show every extreme that they name: `item_lengths`: the item lengths sum to 2048; exactly one item has 1536 tokens, every other at least 128.
All inputs are finite; a program needn't handle non-finite values.
Results may differ from a plain program's by a relative error of at most 0.02.
Values may be sent and summed in bfloat16 or wider, within the bound.
No kernel may reach another device: no remote copies, remote signals or barrier semaphores. Data moves between devices by JAX's collectives and lax.ppermute only.
A program may use at most 384 MiB of HBM per device.

v0:
```python
import math
import jax
import jax.numpy as jnp
from jax import lax
from jax.sharding import PartitionSpec as P

EPS = 1e-06
THETA = 1000000.0
NEG = -1e30


def right_dot(first_matrix, second_matrix):
    return lax.dot_general(
        first_matrix, second_matrix, (((1,), (1,)), ((), ())), preferred_element_type=jnp.float32
    )


def plain_dot(first_matrix, second_matrix):
    return jnp.dot(first_matrix, second_matrix, preferred_element_type=jnp.float32)


def outer_dot(first_matrix, second_matrix):
    return lax.dot_general(
        first_matrix, second_matrix, (((0,), (0,)), ((), ())), preferred_element_type=jnp.float32
    )


def normalize(values, gain_vector):
    inverse = lax.rsqrt(jnp.mean(values * values, axis=-1, keepdims=True) + EPS)
    return (values * inverse * gain_vector, inverse)


def normalize_back(values, inverse, gain_vector, upstream):
    weighted = upstream * gain_vector
    inner_mean = jnp.mean(weighted * values, axis=-1, keepdims=True)
    return (
        inverse * weighted - values * inverse * inverse * inverse * inner_mean,
        values * inverse * upstream,
    )


def rotary_tables(positions, head_width):
    half_width = head_width // 2
    frequency = THETA ** (-2.0 * jnp.arange(half_width, dtype=jnp.float32) / head_width)
    angles = positions.astype(jnp.float32)[:, None] * frequency[None, :]
    return (jnp.cos(angles)[:, None, :], jnp.sin(angles)[:, None, :])


def rotate(values, cosine_table, sine_table):
    half_width = values.shape[-1] // 2
    former = values[..., :half_width]
    latter = values[..., half_width:]
    return jnp.concatenate(
        [former * cosine_table - latter * sine_table, latter * cosine_table + former * sine_table],
        axis=-1,
    )


def item_geometry(item_lengths, first_row, row_count):
    item_ends = jnp.cumsum(item_lengths)
    item_starts = item_ends - item_lengths
    row_index = first_row + jnp.arange(row_count, dtype=jnp.int32)
    begins = jnp.max(
        jnp.where(item_starts[None, :] <= row_index[:, None], item_starts[None, :], 0), axis=1
    )
    return (row_index, begins)


def block_scores(queries, key_block, block_start, row_index, begins, score_scale):
    scores = (
        jnp.einsum("rkgd,skd->kgrs", queries, key_block, preferred_element_type=jnp.float32)
        * score_scale
    )
    key_index = block_start + jnp.arange(key_block.shape[0], dtype=jnp.int32)
    valid = (key_index[None, :] >= begins[:, None]) & (key_index[None, :] <= row_index[:, None])
    return (jnp.where(valid, scores, NEG), valid)


def swiglu(inputs_low, gate_rows, up_rows):
    gate_pre = right_dot(inputs_low, gate_rows)
    up_pre = right_dot(inputs_low, up_rows)
    return (gate_pre, up_pre, (jax.nn.silu(gate_pre) * up_pre).astype(jnp.bfloat16))


def swiglu_back(gate_pre, up_pre, grad_act):
    sigma = jax.nn.sigmoid(gate_pre)
    grad_gate = grad_act * up_pre * sigma * (1.0 + gate_pre * (1.0 - sigma))
    grad_up = grad_act * gate_pre * sigma
    return (grad_gate.astype(jnp.bfloat16), grad_up.astype(jnp.bfloat16))


def shards(
    tokens,
    item_lengths,
    first_gain,
    query_weight,
    key_weight,
    value_weight,
    headgate_weight,
    merge_weight,
    query_norm,
    key_norm,
    second_gain,
    gate_weight,
    up_weight,
    down_weight,
    out_cotangent,
):
    sp_size = lax.axis_size("sp")
    local_rows = tokens.shape[0]
    total_rows = local_rows * sp_size
    head_width = query_norm.shape[0]
    local_heads = query_weight.shape[0] // head_width
    local_groups = key_weight.shape[0] // head_width
    group_size = local_heads // local_groups
    score_scale = 1.0 / math.sqrt(head_width)
    first_row = lax.axis_index("sp") * local_rows
    row_index, begins = item_geometry(item_lengths, first_row, local_rows)
    cosine_table, sine_table = rotary_tables(row_index - begins, head_width)
    last_row = first_row + local_rows - 1
    first_begin = begins[0]
    residual = tokens.astype(jnp.float32)
    first_gain_f = first_gain.astype(jnp.float32)
    second_gain_f = second_gain.astype(jnp.float32)
    query_gain = query_norm.astype(jnp.float32)
    key_gain = key_norm.astype(jnp.float32)
    normed, first_inverse = normalize(residual, first_gain_f)
    normed_low = normed.astype(jnp.bfloat16)
    query_heads = right_dot(normed_low, query_weight).reshape(local_rows, local_heads, head_width)
    key_heads = right_dot(normed_low, key_weight).reshape(local_rows, local_groups, head_width)
    value_low = right_dot(normed_low, value_weight).astype(jnp.bfloat16)
    gate_logit = right_dot(normed_low, headgate_weight)
    query_unit, query_inverse = normalize(query_heads, query_gain)
    key_unit, key_inverse = normalize(key_heads, key_gain)
    queries = (
        rotate(query_unit, cosine_table, sine_table)
        .astype(jnp.bfloat16)
        .reshape(local_rows, local_groups, group_size, head_width)
    )
    keys_low = (
        rotate(key_unit, cosine_table, sine_table)
        .astype(jnp.bfloat16)
        .reshape(local_rows, local_groups * head_width)
    )
    keys_all, values_all = (
        lax.all_gather(keys_low, "sp", axis=0, tiled=True),
        lax.all_gather(value_low, "sp", axis=0, tiled=True),
    )
    block_size = math.gcd(total_rows, 1024)
    block_count = total_rows // block_size
    key_blocks = keys_all.reshape(block_count, block_size, local_groups, head_width)
    value_blocks = values_all.reshape(block_count, block_size, local_groups, head_width)
    block_starts = jnp.arange(block_count, dtype=jnp.int32) * block_size

    def needed(block_start):
        return (block_start <= last_row) & (block_start + block_size > first_begin)

    def first_pass(carried, inputs):
        key_block, value_block, block_start = inputs

        def first_update(current):
            running_max, running_sum = current
            scores, valid = block_scores(
                queries, key_block, block_start, row_index, begins, score_scale
            )
            new_max = jnp.maximum(running_max, jnp.max(scores, axis=-1))
            weights = jnp.where(valid, jnp.exp(scores - new_max[..., None]), 0.0)
            return (
                new_max,
                running_sum * jnp.exp(running_max - new_max) + jnp.sum(weights, axis=-1),
            )

        def first_unchanged(current):
            return current

        return (lax.cond(needed(block_start), first_update, first_unchanged, carried), None)

    start_max = jnp.full((local_groups, group_size, local_rows), NEG, jnp.float32)
    start_sum = jnp.zeros((local_groups, group_size, local_rows), jnp.float32)
    (running_max, running_sum), _ = lax.scan(
        first_pass, (start_max, start_sum), (key_blocks, value_blocks, block_starts)
    )
    log_total = running_max + jnp.log(running_sum)

    def second_pass(carried, inputs):
        key_block, value_block, block_start = inputs

        def second_update(current):
            scores, valid = block_scores(
                queries, key_block, block_start, row_index, begins, score_scale
            )
            probs = jnp.where(valid, jnp.exp(scores - log_total[..., None]), 0.0).astype(
                jnp.bfloat16
            )
            return current + jnp.einsum(
                "kgrs,skd->kgrd", probs, value_block, preferred_element_type=jnp.float32
            )

        def second_unchanged(current):
            return current

        return (lax.cond(needed(block_start), second_update, second_unchanged, carried), None)

    start_acc = jnp.zeros((local_groups, group_size, local_rows, head_width), jnp.float32)
    accumulated, _ = lax.scan(second_pass, start_acc, (key_blocks, value_blocks, block_starts))
    attended = jnp.transpose(accumulated, (2, 0, 1, 3)).reshape(local_rows, local_heads, head_width)
    gate_value = jax.nn.sigmoid(gate_logit)
    gated_low = (
        (attended * gate_value[..., None])
        .astype(jnp.bfloat16)
        .reshape(local_rows, local_heads * head_width)
    )
    attention_out = lax.psum(right_dot(gated_low, merge_weight).astype(jnp.bfloat16), "tp").astype(
        jnp.float32
    )
    hidden = residual + attention_out
    normed_second, second_inverse = normalize(hidden, second_gain_f)
    second_low = normed_second.astype(jnp.bfloat16)
    acts_all = swiglu(lax.all_gather(second_low, "sp", axis=0, tiled=True), gate_weight, up_weight)[
        2
    ]
    branch_part = lax.psum_scatter(
        plain_dot(acts_all, down_weight), "sp", scatter_dimension=0, tiled=True
    )
    branch_out = lax.psum(branch_part.astype(jnp.bfloat16), "tp").astype(jnp.float32)
    layer_output = (hidden + branch_out).astype(jnp.bfloat16)
    grad_out = out_cotangent.astype(jnp.float32)
    stacked_weights = jnp.concatenate([gate_weight, up_weight], axis=0)
    inputs_low = lax.all_gather(second_low, "sp", axis=0, tiled=True)
    grads_low = lax.all_gather(out_cotangent, "sp", axis=0, tiled=True)
    gate_pre, up_pre, act_low = swiglu(inputs_low, gate_weight, up_weight)
    grad_act = right_dot(grads_low, down_weight)
    grad_gate, grad_up = swiglu_back(gate_pre, up_pre, grad_act)
    gate_acc = outer_dot(grad_gate, inputs_low)
    up_acc = outer_dot(grad_up, inputs_low)
    down_acc = outer_dot(act_low, grads_low)
    fold_stacked_grads = jnp.concatenate([grad_gate, grad_up], axis=1)
    second_part = lax.psum_scatter(
        plain_dot(fold_stacked_grads, stacked_weights), "sp", scatter_dimension=0, tiled=True
    )
    grad_second = lax.psum(second_part.astype(jnp.bfloat16), "tp").astype(jnp.float32)
    grad_hidden_norm, second_terms = normalize_back(
        hidden, second_inverse, second_gain_f, grad_second
    )
    hidden_grad = grad_out + grad_hidden_norm
    hidden_low = hidden_grad.astype(jnp.bfloat16)
    merge_grad = outer_dot(hidden_low, gated_low)
    grad_gated = plain_dot(hidden_low, merge_weight).reshape(local_rows, local_heads, head_width)
    grad_attended_low = (grad_gated * gate_value[..., None]).astype(jnp.bfloat16)
    grad_logit_low = (
        jnp.sum(grad_gated * attended, axis=-1) * gate_value * (1.0 - gate_value)
    ).astype(jnp.bfloat16)
    row_delta = jnp.sum(grad_attended_low.astype(jnp.float32) * attended, axis=-1).reshape(
        local_rows, local_groups, group_size
    )
    row_delta = jnp.transpose(row_delta, (1, 2, 0))
    grad_grouped = grad_attended_low.reshape(local_rows, local_groups, group_size, head_width)

    def back_pass(carried, inputs):
        key_block, value_block, block_start = inputs

        def back_update(grad_queries):
            scores, valid = block_scores(
                queries, key_block, block_start, row_index, begins, score_scale
            )
            probs = jnp.where(valid, jnp.exp(scores - log_total[..., None]), 0.0)
            grad_probs = jnp.einsum(
                "rkgd,skd->kgrs", grad_grouped, value_block, preferred_element_type=jnp.float32
            )
            grad_scores = (probs * (grad_probs - row_delta[..., None])).astype(jnp.bfloat16)
            grad_queries = (
                grad_queries
                + jnp.einsum(
                    "kgrs,skd->rkgd", grad_scores, key_block, preferred_element_type=jnp.float32
                )
                * score_scale
            )
            grad_keys = (
                jnp.einsum(
                    "kgrs,rkgd->skd", grad_scores, queries, preferred_element_type=jnp.float32
                )
                * score_scale
            )
            grad_values = jnp.einsum(
                "kgrs,rkgd->skd",
                probs.astype(jnp.bfloat16),
                grad_grouped,
                preferred_element_type=jnp.float32,
            )
            return (grad_queries, (grad_keys, grad_values))

        def skipped(grad_queries):
            empty = jnp.zeros((block_size, local_groups, head_width), jnp.float32)
            return (grad_queries, (empty, empty))

        return lax.cond(needed(block_start), back_update, skipped, carried)

    start_queries = jnp.zeros((local_rows, local_groups, group_size, head_width), jnp.float32)
    grad_queries, (key_parts, value_parts) = lax.scan(
        back_pass, start_queries, (key_blocks, value_blocks, block_starts)
    )
    key_terms = key_parts.reshape(total_rows, local_groups * head_width)
    value_terms = value_parts.reshape(total_rows, local_groups * head_width)
    key_sum, value_sum = (
        lax.psum_scatter(key_terms, "sp", scatter_dimension=0, tiled=True),
        lax.psum_scatter(value_terms, "sp", scatter_dimension=0, tiled=True),
    )
    grad_query_unit = rotate(
        grad_queries.reshape(local_rows, local_heads, head_width), cosine_table, -sine_table
    )
    grad_query_raw, query_gain_terms = normalize_back(
        query_heads, query_inverse, query_gain, grad_query_unit
    )
    grad_key_unit = rotate(
        key_sum.reshape(local_rows, local_groups, head_width), cosine_table, -sine_table
    )
    grad_key_raw, key_gain_terms = normalize_back(key_heads, key_inverse, key_gain, grad_key_unit)
    query_low = grad_query_raw.reshape(local_rows, local_heads * head_width).astype(jnp.bfloat16)
    key_low = grad_key_raw.reshape(local_rows, local_groups * head_width).astype(jnp.bfloat16)
    value_grad_low = value_sum.astype(jnp.bfloat16)
    query_grad = outer_dot(query_low, normed_low)
    key_grad = outer_dot(key_low, normed_low)
    value_grad = outer_dot(value_grad_low, normed_low)
    headgate_grad = outer_dot(grad_logit_low, normed_low)
    input_part = (
        plain_dot(query_low, query_weight)
        + plain_dot(key_low, key_weight)
        + plain_dot(value_grad_low, value_weight)
        + plain_dot(grad_logit_low, headgate_weight)
    )
    input_sum, query_gain_sum, key_gain_sum = (
        lax.psum(input_part.astype(jnp.bfloat16), "tp").astype(jnp.float32),
        lax.psum(jnp.sum(query_gain_terms, axis=(0, 1)).astype(jnp.bfloat16), "tp").astype(
            jnp.float32
        ),
        lax.psum(jnp.sum(key_gain_terms, axis=(0, 1)).astype(jnp.bfloat16), "tp").astype(
            jnp.float32
        ),
    )
    grad_residual_norm, first_terms = normalize_back(
        residual, first_inverse, first_gain_f, input_sum
    )
    input_grad = hidden_grad + grad_residual_norm
    reduced = lax.psum(
        (
            query_grad,
            key_grad,
            value_grad,
            headgate_grad,
            merge_grad,
            query_gain_sum,
            key_gain_sum,
            jnp.sum(first_terms, axis=0),
            jnp.sum(second_terms, axis=0),
        ),
        "sp",
    )
    return (
        layer_output,
        input_grad,
        reduced[7],
        reduced[0],
        reduced[1],
        reduced[2],
        reduced[3],
        reduced[4],
        reduced[5],
        reduced[6],
        reduced[8],
        gate_acc,
        up_acc,
        down_acc,
    )


def solution(mesh):
    return jax.shard_map(
        shards,
        mesh=mesh,
        in_specs=(
            P("sp", None),
            P(),
            P(),
            P("tp", None),
            P("tp", None),
            P("tp", None),
            P("tp", None),
            P(None, "tp"),
            P(),
            P(),
            P(),
            P(("tp", "sp"), None),
            P(("tp", "sp"), None),
            P(("tp", "sp"), None),
            P("sp", None),
        ),
        out_specs=(
            P("sp", None),
            P("sp", None),
            P(),
            P("tp", None),
            P("tp", None),
            P("tp", None),
            P("tp", None),
            P(None, "tp"),
            P(),
            P(),
            P(),
            P(("tp", "sp"), None),
            P(("tp", "sp"), None),
            P(("tp", "sp"), None),
        ),
        check_vma=False,
    )
```

profile of v0, /device:TPU:0, one launch (start us, length us, event | category | flops | bytes accessed | tf_op | source)
XLA Modules:
  0.0 1403.6 jit_solution(12109485041984418641)
XLA Ops:
  24.9 32.0 %all-gather.7.cloned.1.call-done = bf16[2048,512]{1,0:T(8,128)(2,1)} async-done(((bf16[128,512]{1,0:T(8,128)(2,1)}), bf16[2048,512]{1,0:T(8,128)(2,1)}) %all-gather.7.cloned.1.call-update) | async-done | bytes 2097168 | tf_op jit(solution)/shard_map/all_gather | solution.py:147
  64.0 35.8 %all-gather.5.cloned.1.call-done = bf16[2048,512]{1,0:T(8,128)(2,1)} async-done(((bf16[128,512]{1,0:T(8,128)(2,1)}), bf16[2048,512]{1,0:T(8,128)(2,1)}) %all-gather.5.cloned.1.call-update) | async-done | bytes 2097168 | tf_op jit(solution)/shard_map/all_gather | solution.py:146
  106.9 7.9 while.45
  114.9 8.3 while.46
  126.1 4.5 convolution_convert_fusion
  131.5 35.0 %all-reduce.9.cloned.1.call-done = bf16[128,2048]{1,0:T(8,128)(2,1)} async-done(((bf16[128,2048]{1,0:T(8,128)(2,1)}), bf16[128,2048]{1,0:T(8,128)(2,1)}) %all-reduce.9.cloned.1.call-update) | async-done | bytes 524304 | tf_op jit(solution)/shard_map/psum | solution.py:213
  170.0 73.8 %all-gather.11.cloned.1.call-done = bf16[2048,2048]{1,0:T(8,128)(2,1)} async-done(((bf16[128,2048]{1,0:T(8,128)(2,1)}), bf16[2048,2048]{1,0:T(8,128)(2,1)}) %all-gather.11.cloned.1.call-update) | async-done | bytes 8388624 | tf_op jit(solution)/shard_map/all_gather | solution.py:230
  243.7 7.6 fusion.129
  251.3 68.4 %all-gather.9.cloned.1.call-done = bf16[2048,2048]{1,0:T(8,128)(2,1)} async-done(((bf16[128,2048]{1,0:T(8,128)(2,1)}), bf16[2048,2048]{1,0:T(8,128)(2,1)}) %all-gather.9.cloned.1.call-update) | async-done | bytes 8388624 | tf_op jit(solution)/shard_map/all_gather | solution.py:219
  319.7 6.6 fusion.127
  331.8 8.2 fusion.61
  340.1 176.9 %reduce-scatter.7.cloned.1.call-done = f32[128,2048]{1,0:T(8,128)} async-done(((f32[2048,2048]{1,0:T(8,128)}), f32[128,2048]{1,0:T(8,128)}) %reduce-scatter.7.cloned.1.call-update) | async-done | bytes 1048592 | tf_op jit(solution)/shard_map/reduce_scatter | solution.py:238
  519.2 9.6 fusion.128
  529.1 18.5 %all-reduce.11.cloned.1.call-done = bf16[128,2048]{1,0:T(8,128)(2,1)} async-done(((bf16[128,2048]{1,0:T(8,128)(2,1)}), bf16[128,2048]{1,0:T(8,128)(2,1)}) %all-reduce.11.cloned.1.call-update) | async-done | bytes 524304 | tf_op jit(solution)/shard_map/psum | solution.py:241
  559.1 31.8 %while.47 = (s32[]{:T(128)}, f32[128,4,2,128]{3,0,2,1:T(8,128)S(1)}, f32[2,1024,4,128]{3,2,1,0:T(4,128)}, f32[2,1024,4,128]{3,2,1,0:T(4,128)}, s32[2]{0:T(128)S(...) while((s32[]{:T(128)}, ...), condition=%wide.region_26.27_spmd.clone, body=%wide.region_23.26_spmd.clone.sunk | while | flops 1355940992 | bytes 54943664 | solution.py:299
  561.0 10.3 conditional.11
  571.4 7.7 copy_dynamic-update-slice_fusion.3
  584.0 6.9 copy_dynamic-update-slice_fusion.3
  590.9 4.6 copy.160
  595.6 4.7 copy.159
  602.2 128.2 %reduce-scatter.5.cloned.1.call-done = f32[128,2048]{1,0:T(8,128)} async-done(((f32[2048,2048]{1,0:T(8,128)}), f32[128,2048]{1,0:T(8,128)}) %reduce-scatter.5.cloned.1.call-update) | async-done | bytes 1048592 | tf_op jit(solution)/shard_map/reduce_scatter | solution.py:222
  741.5 4.9 fusion.102
  746.4 59.9 %reduce-scatter.9.cloned.1.call-done = f32[128,512]{1,0:T(8,128)} async-done(((f32[2048,512]{1,0:T(8,128)}), f32[128,512]{1,0:T(8,128)}) %reduce-scatter.9.cloned.1.call-update) | async-done | bytes 262160 | tf_op jit(solution)/shard_map/reduce_scatter | solution.py:305
  814.7 67.7 %reduce-scatter.11.cloned.1.call-done = f32[128,512]{1,0:T(8,128)} async-done(((f32[2048,512]{1,0:T(8,128)}), f32[128,512]{1,0:T(8,128)}) %reduce-scatter.11.cloned.1.call-update) | async-done | bytes 262160 | tf_op jit(solution)/shard_map/reduce_scatter | solution.py:306
  886.2 5.5 fusion.118
  897.4 6.8 fusion.133
  904.2 6.5 fusion.131
  913.8 5.0 all-reduce.2
  918.8 6.7 all-reduce.15.cloned.1.call-done
  927.2 64.4 %all-reduce = (f32[2048]{0:T(1024)}, f32[128]{0:T(128)}, f32[128]{0:T(128)}, f32[2048]{0:T(1024)}) all-reduce(f32[2048]{0:T(1024)S(1)} %get-tuple-element.661, bf16[128]{0:T(256)(128)(2,1)S(1)} %get-tuple-element.744, bf16[128]{0:T(256)(128)(2,1)S(1)} %get-tuple-element.745, ...), channel_id=1, replica_groups=mesh['tp'=2,'sp'=16] {'sp'}, use_global_device_ids=true, to_apply=%region_35.36 | all-reduce | flops 4352 | bytes 34304 | tf_op jit(solution)/shard_map/psum | solution.py:344
  995.2 382.0 %all-reduce.13.cloned.1.call-done = (f32[1024,2048]{1,0:T(8,128)}, f32[512,2048]{1,0:T(8,128)}, f32[512,2048]{1,0:T(8,128)}, f32[8,2048]{1,0:T(8,128)}, f32[2048,1024]{1,0:T(8,128)}) async-done(((f32[1024,2048]{1,0:T(8,128)}, f32[512,2048]{1,0:T(8,128)}, f32[512,2048]{1,0:T(8,128)}, f32[8,2048]{1,0:T(8,128)}, f32[2048,1024]{1,0:T(8,128)}), (f32[1024,2048]{1,0:T(8,128)}, f32[512,2048]{1,0:T(8,128)}, ...) | async-done | bytes 25231376 | tf_op jit(solution)/shard_map/psum | solution.py:344
  1377.2 8.0 copy.216
  (318 shorter events, 144.7 us)
Async XLA Ops:
  7.2 49.6 %all-gather.7.cloned.1.call-start = ((), (), s32[]{:S(2)}) async-start(), calls=%async_computation.5 | async-start | bytes 2228224 | tf_op jit(solution)/shard_map/all_gather | solution.py:147
  8.6 15.9 %copy-start.47 = (f32[128]{0:T(128)}, f32[128]{0:T(128)S(1)}, u32[]{:S(2)}) copy-start(f32[128]{0:T(128)S(1)} %add_rsqrt_fusion.3) | copy-start | bytes 1540
  9.3 15.2 %copy-start.38 = (f32[2048]{0:T(1024)}, f32[2048]{0:T(1024)S(1)}, u32[]{:S(2)}) copy-start(f32[2048]{0:T(1024)S(1)} %convert_element_type.143) | copy-start | bytes 24580
  9.3 9.0 copy-start.71
  9.3 9.0 copy-start.1
  12.7 87.1 %all-gather.5.cloned.1.call-start = ((), (), s32[]{:S(2)}) async-start(), calls=%async_computation.4 | async-start | bytes 2228224 | tf_op jit(solution)/shard_map/all_gather | solution.py:146
  18.3 148.3 %all-reduce.9.cloned.1.call-start = ((), (), s32[]{:S(2)}) async-start(), calls=%async_computation.6 | async-start | bytes 1048576 | tf_op jit(solution)/shard_map/psum | solution.py:213
  24.9 530.5 %copy-start.42 = (f32[128,8]{0,1:T(8,128)}, f32[128,8]{0,1:T(8,128)S(1)}, u32[]{:S(2)}) copy-start(f32[128,8]{0,1:T(8,128)S(1)} %fusion.76) | copy-start | bytes 12292
  125.3 44.6 %copy-start.10 = (f32[4,2,128,128]{2,3,1,0:T(8,128)}, f32[4,2,128,128]{2,3,1,0:T(8,128)S(1)}, u32[]{:S(2)}) copy-start(f32[4,2,128,128]{2,3,1,0:T(8,128)S(1)} %copy.82) | copy-start | bytes 1572868
  130.7 113.1 %all-gather.11.cloned.1.call-start = ((), (), s32[]{:S(2)}) async-start(), calls=%async_computation.9 | async-start | bytes 8912896 | tf_op jit(solution)/shard_map/all_gather | solution.py:230
  131.3 188.4 %all-gather.9.cloned.1.call-start = ((), (), s32[]{:S(2)}) async-start(), calls=%async_computation.7 | async-start | bytes 8912896 | tf_op jit(solution)/shard_map/all_gather | solution.py:219
  167.8 381.9 %copy-start.53 = (f32[128]{0:T(128)}, f32[128]{0:T(128)S(1)}, u32[]{:S(2)}) copy-start(f32[128]{0:T(128)S(1)} %add_rsqrt_fusion.2) | copy-start | bytes 1540
  169.9 347.1 %reduce-scatter.7.cloned.1.call-start = ((), (), s32[]{:S(2)}) async-start(), calls=%async_computation.10 | async-start | bytes 17825792 | tf_op jit(solution)/shard_map/reduce_scatter | solution.py:238
  340.1 207.6 %all-reduce.11.cloned.1.call-start = ((), (), s32[]{:S(2)}) async-start(), calls=%async_computation.11 | async-start | bytes 1048576 | tf_op jit(solution)/shard_map/psum | solution.py:241
  519.2 211.2 %reduce-scatter.5.cloned.1.call-start = ((), (), s32[]{:S(2)}) async-start(), calls=%async_computation.8 | async-start | bytes 17825792 | tf_op jit(solution)/shard_map/reduce_scatter | solution.py:222
  528.8 18.9 %copy-start.4 = (bf16[128,2048]{1,0:T(8,128)(2,1)S(1)}, bf16[128,2048]{1,0:T(8,128)(2,1)}, u32[]{:S(2)}) copy-start(bf16[128,2048]{1,0:T(8,128)(2,1)} %all-reduce.9.cloned.1.call-done) | copy-start | bytes 1572868
  528.8 277.5 %reduce-scatter.9.cloned.1.call-start = ((), (), s32[]{:S(2)}) async-start(), calls=%async_computation.12 | async-start | bytes 4456448 | tf_op jit(solution)/shard_map/reduce_scatter | solution.py:305
  549.8 9.3 copy-start.68
  549.8 9.3 copy-start.73
  595.6 286.9 %reduce-scatter.11.cloned.1.call-start = ((), (), s32[]{:S(2)}) async-start(), calls=%async_computation.13 | async-start | bytes 4456448 | tf_op jit(solution)/shard_map/reduce_scatter | solution.py:306
  600.3 134.8 %copy-start.43 = (f32[128,8]{0,1:T(8,128)S(1)}, f32[128,8]{0,1:T(8,128)}, u32[]{:S(2)}) copy-start(f32[128,8]{0,1:T(8,128)} %copy-done.42) | copy-start | bytes 12292
  600.3 135.1 %copy-start.26 = (f32[128,64]{1,0:T(8,128)S(1)}, f32[128,64]{1,0:T(8,128)}, u32[]{:S(2)}) copy-start(f32[128,64]{1,0:T(8,128)} %copy-done.25) | copy-start | bytes 98308
  600.3 135.1 %copy-start.34 = (f32[128,64]{1,0:T(8,128)S(1)}, f32[128,64]{1,0:T(8,128)}, u32[]{:S(2)}) copy-start(f32[128,64]{1,0:T(8,128)} %get-tuple-element.777) | copy-start | bytes 98308
  600.3 325.2 %all-reduce.15.cloned.1.call-start = ((), (), s32[]{:S(2)}) async-start(), calls=%async_computation.15 | async-start | bytes 2097152 | tf_op jit(solution)/shard_map/psum | solution.py:225
  741.5 67.8 %copy-start.17 = (f32[128,4,128]{2,1,0:T(4,128)S(1)}, f32[128,4,128]{2,1,0:T(4,128)}, u32[]{:S(2)}) copy-start(f32[128,4,128]{2,1,0:T(4,128)} %copy-done.16) | copy-start | bytes 786436
  814.7 71.5 %copy-start.20 = (bf16[128,1024]{1,0:T(8,128)(2,1)S(1)}, bf16[128,1024]{1,0:T(8,128)(2,1)}, u32[]{:S(2)}) copy-start(bf16[128,1024]{1,0:T(8,128)(2,1)} %copy-done.19) | copy-start | bytes 786436
  886.0 491.2 %all-reduce.13.cloned.1.call-start = ((), (), s32[]{:S(2)}) async-start(), calls=%async_computation.14 | async-start | bytes 50462720 | tf_op jit(solution)/shard_map/psum | solution.py:344
  897.4 13.3 slice-start.2
  910.7 14.8 %copy-start.50 = (f32[128]{0:T(128)S(1)}, f32[128]{0:T(128)}, u32[]{:S(2)}) copy-start(f32[128]{0:T(128)} %copy-done.47) | copy-start | bytes 1540
  910.7 16.4 %copy-start.44 = (f32[2048]{0:T(1024)S(1)}, f32[2048]{0:T(1024)}, u32[]{:S(2)}) copy-start(f32[2048]{0:T(1024)} %get-tuple-element.659) | copy-start | bytes 24580
  910.7 80.8 %copy-start.55 = (f32[128]{0:T(128)S(1)}, f32[128]{0:T(128)}, u32[]{:S(2)}) copy-start(f32[128]{0:T(128)} %copy-done.53) | copy-start | bytes 1540
  910.8 80.8 %copy-start.61 = (f32[128]{0:T(128)S(1)}, f32[128]{0:T(128)}, u32[]{:S(2)}) copy-start(f32[128]{0:T(128)} %copy-done.59) | copy-start | bytes 1540
  (59 other events, 240.7 us)
Sparse Core Ops, SparseCore 0:
  12.8 44.0 all-gather.6
  59.6 40.1 all-gather.4
  130.8 35.7 all-reduce.8
  168.8 74.8 all-gather.10
  246.5 73.1 all-gather.8
  340.2 176.8 reduce-scatter.6
  520.0 27.5 all-reduce.10
  551.7 178.5 reduce-scatter.4
  734.8 71.4 reduce-scatter.8
  811.0 71.3 reduce-scatter.10
  886.1 39.4 all-reduce.14
  932.2 444.9 all-reduce.12
where the time goes:
time: 1410 us; the launch traced here: 1400 us
  waiting for transfers between devices  1090 us (77%)
  matrix products  109 us (8%)
  local copies, waits for them, and re-layouts  80.7 us (6%)
  blocking collectives  69.4 us (5%)
  other arithmetic  33.8 us (2%)
  between operations  15.4 us (1%)
    psum x1, waiting for transfers between devices, shards(): lax.psum((query_grad, key_grad, value_grad, headgate_grad, merge_grad, qu...  382 us
    reduce_scatter x1, waiting for transfers between devices, shards(): lax.psum_scatter(plain_dot(fold_stacked_grads, stacked_weights), 'sp', sc...  177 us
    reduce_scatter x1, waiting for transfers between devices, shards(): lax.psum_scatter(plain_dot(acts_all, down_weight), 'sp', scatter_dimensio...  128 us
    all_gather x1, waiting for transfers between devices, shards(): grads_low = lax.all_gather(out_cotangent, 'sp', axis=0, tiled=True)  73.8 us
    all_gather x1, waiting for transfers between devices, shards(): lax.all_gather(second_low, 'sp', axis=0, tiled=True)  68.4 us
    reduce_scatter x1, waiting for transfers between devices, shards(): lax.psum_scatter(value_terms, 'sp', scatter_dimension=0, tiled=True)  67.7 us
    psum x1, blocking collectives, shards(): lax.psum((query_grad, key_grad, value_grad, headgate_grad, merge_grad, qu...  64.4 us
    reduce_scatter x1, waiting for transfers between devices, shards(): lax.psum_scatter(key_terms, 'sp', scatter_dimension=0, tiled=True)  59.9 us
  transfers between devices with their start and end apart: 12, of which 12 were waited for; matrix products, arithmetic and copies ran while one was open for 10% of the time, Pallas kernels for 0%

commit v1 on v0

--- a/solution.py
+++ b/solution.py
@@ -7,6 +7,12 @@
 EPS = 1e-06
 THETA = 1000000.0
 NEG = -1e30
+
+
+def _put_shelves(w_in, xs):
+    return jnp.split(
+        lax.all_gather(jnp.concatenate([xs, w_in], 1), "sp", axis=0, tiled=True), [xs.shape[1]], 1
+    )
 
 
 def right_dot(first_matrix, second_matrix):
@@ -226,8 +232,7 @@
     layer_output = (hidden + branch_out).astype(jnp.bfloat16)
     grad_out = out_cotangent.astype(jnp.float32)
     stacked_weights = jnp.concatenate([gate_weight, up_weight], axis=0)
-    inputs_low = lax.all_gather(second_low, "sp", axis=0, tiled=True)
-    grads_low = lax.all_gather(out_cotangent, "sp", axis=0, tiled=True)
+    inputs_low, grads_low = _put_shelves(out_cotangent, second_low)
     gate_pre, up_pre, act_low = swiglu(inputs_low, gate_weight, up_weight)
     grad_act = right_dot(grads_low, down_weight)
     grad_gate, grad_up = swiglu_back(gate_pre, up_pre, grad_act)

time: 1410 us -> 1450 us (1.028)
  waiting for transfers between devices: 1090 us -> 1110 us
  matrix products: 109 us -> 126 us
    all_gather x1, waiting for transfers between devices: 73.8 us -> 126 us  [_put_shelves(): lax.all_gather(jnp.concatenate([xs, w_in], 1), 'sp', axis=0, tiled=True)]
    all_gather x1, waiting for transfers between devices: 68.4 us -> 47.9 us  [shards(): lax.all_gather(second_low, 'sp', axis=0, tiled=True)]
    dot_general x8 -> x9, matrix products: 32.2 us -> 39.7 us  [right_dot(): lax.dot_general(first_matrix, second_matrix, (((1,), (1,)), ((), ())), pr...]
    unnamed x165 -> x173, local copies, waits for them, and re-layouts: 44.1 us -> 44.9 us
  transfers between devices with their start and end apart: 12 -> 12, of which waited for: 12 -> 12; matrix products, arithmetic and copies ran while one was open for 10% -> 12% of each run, Pallas kernels for 0% -> 0%
where the time goes in v1:
time: 1450 us; the launch traced here: 1440 us
  waiting for transfers between devices  1110 us (77%)
  matrix products  126 us (9%)
  local copies, waits for them, and re-layouts  81.5 us (6%)
  blocking collectives  69.3 us (5%)
  other arithmetic  35.8 us (2%)
  between operations  15.7 us (1%)
    psum x1, waiting for transfers between devices, shards(): lax.psum((query_grad, key_grad, value_grad, headgate_grad, merge_grad, qu...  382 us
    reduce_scatter x1, waiting for transfers between devices, shards(): lax.psum_scatter(plain_dot(fold_stacked_grads, stacked_weights), 'sp', sc...  174 us
    reduce_scatter x1, waiting for transfers between devices, shards(): lax.psum_scatter(plain_dot(acts_all, down_weight), 'sp', scatter_dimensio...  128 us
    all_gather x1, waiting for transfers between devices, _put_shelves(): lax.all_gather(jnp.concatenate([xs, w_in], 1), 'sp', axis=0, tiled=True)  126 us
    reduce_scatter x1, waiting for transfers between devices, shards(): lax.psum_scatter(value_terms, 'sp', scatter_dimension=0, tiled=True)  67.7 us
    psum x1, blocking collectives, shards(): lax.psum((query_grad, key_grad, value_grad, headgate_grad, merge_grad, qu...  64.4 us
    reduce_scatter x1, waiting for transfers between devices, shards(): lax.psum_scatter(key_terms, 'sp', scatter_dimension=0, tiled=True)  59.9 us
    all_gather x1, waiting for transfers between devices, shards(): lax.all_gather(second_low, 'sp', axis=0, tiled=True)  47.9 us
  transfers between devices with their start and end apart: 12, of which 12 were waited for; matrix products, arithmetic and copies ran while one was open for 12% of the time, Pallas kernels for 0%

profile of v1, /device:TPU:0, one launch (start us, length us, event | category | flops | bytes accessed | tf_op | source)
XLA Modules:
  0.0 1443.8 jit_solution(9714655518298584536)
XLA Ops:
  24.8 32.0 %all-gather.7.cloned.1.call-done = bf16[2048,512]{1,0:T(8,128)(2,1)} async-done(((bf16[128,512]{1,0:T(8,128)(2,1)}), bf16[2048,512]{1,0:T(8,128)(2,1)}) %all-gather.7.cloned.1.call-update) | async-done | bytes 2097168 | tf_op jit(solution)/shard_map/all_gather | solution.py:153
  64.0 35.8 %all-gather.5.cloned.1.call-done = bf16[2048,512]{1,0:T(8,128)(2,1)} async-done(((bf16[128,512]{1,0:T(8,128)(2,1)}), bf16[2048,512]{1,0:T(8,128)(2,1)}) %all-gather.5.cloned.1.call-update) | async-done | bytes 2097168 | tf_op jit(solution)/shard_map/all_gather | solution.py:152
  106.9 7.9 while.45
  114.8 8.3 while.46
  131.8 35.4 %all-reduce.9.cloned.1.call-done = bf16[128,2048]{1,0:T(8,128)(2,1)} async-done(((bf16[128,2048]{1,0:T(8,128)(2,1)}), bf16[128,2048]{1,0:T(8,128)(2,1)}) %all-reduce.9.cloned.1.call-update) | async-done | bytes 524304 | tf_op jit(solution)/shard_map/psum | solution.py:219
  173.4 126.4 %all-gather.11.cloned.1.call-done = bf16[2048,4096]{1,0:T(8,128)(2,1)} async-done(((bf16[128,4096]{1,0:T(8,128)(2,1)}), bf16[2048,4096]{1,0:T(8,128)(2,1)}) %all-gather.11.cloned.1.call-update) | async-done | bytes 16777232 | tf_op jit(solution)/shard_map/all_gather | solution.py:14
  299.8 6.6 fusion.70
  306.4 7.4 fusion.62
  319.4 8.2 fusion.75
  327.8 47.9 %all-gather.9.cloned.1.call-done = bf16[2048,2048]{1,0:T(8,128)(2,1)} async-done(((bf16[128,2048]{1,0:T(8,128)(2,1)}), bf16[2048,2048]{1,0:T(8,128)(2,1)}) %all-gather.9.cloned.1.call-update) | async-done | bytes 8388624 | tf_op jit(solution)/shard_map/all_gather | solution.py:225
  375.7 7.6 fusion.150
  383.3 173.8 %reduce-scatter.7.cloned.1.call-done = f32[128,2048]{1,0:T(8,128)} async-done(((f32[2048,2048]{1,0:T(8,128)}), f32[128,2048]{1,0:T(8,128)}) %reduce-scatter.7.cloned.1.call-update) | async-done | bytes 1048592 | tf_op jit(solution)/shard_map/reduce_scatter | solution.py:243
  559.2 15.2 %fusion.74 = f32[2048,2048]{1,0:T(8,128)} fusion(bf16[192,2048]{1,0:T(8,128)(2,1)} %param.40, bf16[2048,2048]{1,0:T(8,128)(2,1)} %all-gather.9.cloned.1.call-done, bf16[192,2048]{1,0:T(8,128)(2,1)} %param.39, f32[2048,192]{0,1:T(8,128)} %fusion.150), kind=kOutput, calls=%fused_computation.91 | convolution fusion | flops 3223584768 | bytes 28311552 | tf_op jit(solution)/shard_map/dot_general | solution.py:25
  574.7 12.9 all-reduce.11.cloned.1.call-done
  599.1 31.8 %while.47 = (s32[]{:T(128)}, f32[128,4,2,128]{3,0,2,1:T(8,128)S(1)}, f32[2,1024,4,128]{3,2,1,0:T(4,128)}, f32[2,1024,4,128]{3,2,1,0:T(4,128)}, s32[2]{0:T(128)S(...) while((s32[]{:T(128)}, ...), condition=%wide.region_26.27_spmd.clone, body=%wide.region_23.26_spmd.clone.sunk | while | flops 1355940992 | bytes 54943664 | solution.py:304
  601.0 10.3 conditional.11
  611.3 7.7 copy_dynamic-update-slice_fusion.3
  623.9 6.9 copy_dynamic-update-slice_fusion.3
  630.8 4.6 copy.160
  635.6 4.7 copy.159
  642.1 128.3 %reduce-scatter.5.cloned.1.call-done = f32[128,2048]{1,0:T(8,128)} async-done(((f32[2048,2048]{1,0:T(8,128)}), f32[128,2048]{1,0:T(8,128)}) %reduce-scatter.5.cloned.1.call-update) | async-done | bytes 1048592 | tf_op jit(solution)/shard_map/reduce_scatter | solution.py:228
  781.5 4.8 fusion.123
  786.4 59.9 %reduce-scatter.9.cloned.1.call-done = f32[128,512]{1,0:T(8,128)} async-done(((f32[2048,512]{1,0:T(8,128)}), f32[128,512]{1,0:T(8,128)}) %reduce-scatter.9.cloned.1.call-update) | async-done | bytes 262160 | tf_op jit(solution)/shard_map/reduce_scatter | solution.py:310
  854.7 67.7 %reduce-scatter.11.cloned.1.call-done = f32[128,512]{1,0:T(8,128)} async-done(((f32[2048,512]{1,0:T(8,128)}), f32[128,512]{1,0:T(8,128)}) %reduce-scatter.11.cloned.1.call-update) | async-done | bytes 262160 | tf_op jit(solution)/shard_map/reduce_scatter | solution.py:311
  926.3 5.5 fusion.141
  937.5 6.7 fusion.66
  944.2 6.5 fusion.64
  950.8 6.9 fusion.60
  957.7 5.0 all-reduce.2
  967.2 64.4 %all-reduce = (f32[2048]{0:T(1024)}, f32[128]{0:T(128)}, f32[128]{0:T(128)}, f32[2048]{0:T(1024)}) all-reduce(f32[2048]{0:T(1024)S(1)} %get-tuple-element.661, bf16[128]{0:T(256)(128)(2,1)S(1)} %get-tuple-element.744, bf16[128]{0:T(256)(128)(2,1)S(1)} %get-tuple-element.745, ...), channel_id=1, replica_groups=mesh['tp'=2,'sp'=16] {'sp'}, use_global_device_ids=true, to_apply=%region_35.36 | all-reduce | flops 4352 | bytes 34304 | tf_op jit(solution)/shard_map/psum | solution.py:349
  1035.1 382.1 %all-reduce.13.cloned.1.call-done = (f32[1024,2048]{1,0:T(8,128)}, f32[512,2048]{1,0:T(8,128)}, f32[512,2048]{1,0:T(8,128)}, f32[8,2048]{1,0:T(8,128)}, f32[2048,1024]{1,0:T(8,128)}) async-done(((f32[1024,2048]{1,0:T(8,128)}, f32[512,2048]{1,0:T(8,128)}, f32[512,2048]{1,0:T(8,128)}, f32[8,2048]{1,0:T(8,128)}, f32[2048,1024]{1,0:T(8,128)}), (f32[1024,2048]{1,0:T(8,128)}, f32[512,2048]{1,0:T(8,128)}, ...) | async-done | bytes 25231376 | tf_op jit(solution)/shard_map/psum | solution.py:349
  1417.2 8.0 copy.216
  (328 shorter events, 152.2 us)
Async XLA Ops:
  7.2 49.6 %all-gather.7.cloned.1.call-start = ((), (), s32[]{:S(2)}) async-start(), calls=%async_computation.5 | async-start | bytes 2228224 | tf_op jit(solution)/shard_map/all_gather | solution.py:153
  8.6 15.9 %copy-start.48 = (f32[128]{0:T(128)}, f32[128]{0:T(128)S(1)}, u32[]{:S(2)}) copy-start(f32[128]{0:T(128)S(1)} %add_rsqrt_fusion.3) | copy-start | bytes 1540
  9.3 15.2 %copy-start.39 = (f32[2048]{0:T(1024)}, f32[2048]{0:T(1024)S(1)}, u32[]{:S(2)}) copy-start(f32[2048]{0:T(1024)S(1)} %convert_element_type.145) | copy-start | bytes 24580
  9.3 9.0 copy-start.1
  12.7 87.1 %all-gather.5.cloned.1.call-start = ((), (), s32[]{:S(2)}) async-start(), calls=%async_computation.4 | async-start | bytes 2228224 | tf_op jit(solution)/shard_map/all_gather | solution.py:152
  18.3 149.0 %all-reduce.9.cloned.1.call-start = ((), (), s32[]{:S(2)}) async-start(), calls=%async_computation.6 | async-start | bytes 1048576 | tf_op jit(solution)/shard_map/psum | solution.py:219
  24.8 570.5 %copy-start.43 = (f32[128,8]{0,1:T(8,128)}, f32[128,8]{0,1:T(8,128)S(1)}, u32[]{:S(2)}) copy-start(f32[128,8]{0,1:T(8,128)S(1)} %fusion.95) | copy-start | bytes 12292
  126.8 43.8 %copy-start.8 = (bf16[128,2048]{1,0:T(8,128)(2,1)S(1)}, bf16[128,2048]{1,0:T(8,128)(2,1)}, u32[]{:S(2)}) copy-start(bf16[128,2048]{1,0:T(8,128)(2,1)} %param.41) | copy-start | bytes 1572868
  131.4 168.4 %all-gather.11.cloned.1.call-start = ((), (), s32[]{:S(2)}) async-start(), calls=%async_computation.9 | async-start | bytes 17825792 | tf_op jit(solution)/shard_map/all_gather | solution.py:14
  168.6 421.2 %copy-start.54 = (f32[128]{0:T(128)}, f32[128]{0:T(128)S(1)}, u32[]{:S(2)}) copy-start(f32[128]{0:T(128)S(1)} %add_rsqrt_fusion.2) | copy-start | bytes 1540
  172.7 203.0 %all-gather.9.cloned.1.call-start = ((), (), s32[]{:S(2)}) async-start(), calls=%async_computation.7 | async-start | bytes 8912896 | tf_op jit(solution)/shard_map/all_gather | solution.py:225
  173.3 383.7 %reduce-scatter.7.cloned.1.call-start = ((), (), s32[]{:S(2)}) async-start(), calls=%async_computation.10 | async-start | bytes 17825792 | tf_op jit(solution)/shard_map/reduce_scatter | solution.py:243
  299.8 14.0 slice-start.2
  299.8 14.0 slice-start.3
  327.7 259.9 %all-reduce.11.cloned.1.call-start = ((), (), s32[]{:S(2)}) async-start(), calls=%async_computation.11 | async-start | bytes 1048576 | tf_op jit(solution)/shard_map/psum | solution.py:246
  559.2 211.2 %reduce-scatter.5.cloned.1.call-start = ((), (), s32[]{:S(2)}) async-start(), calls=%async_computation.8 | async-start | bytes 17825792 | tf_op jit(solution)/shard_map/reduce_scatter | solution.py:228
  574.5 13.2 copy-start.4
  574.5 271.8 %reduce-scatter.9.cloned.1.call-start = ((), (), s32[]{:S(2)}) async-start(), calls=%async_computation.12 | async-start | bytes 4456448 | tf_op jit(solution)/shard_map/reduce_scatter | solution.py:310
  589.8 9.3 copy-start.69
  589.8 9.3 copy-start.73
  635.5 286.9 %reduce-scatter.11.cloned.1.call-start = ((), (), s32[]{:S(2)}) async-start(), calls=%async_computation.13 | async-start | bytes 4456448 | tf_op jit(solution)/shard_map/reduce_scatter | solution.py:311
  640.3 134.9 %copy-start.44 = (f32[128,8]{0,1:T(8,128)S(1)}, f32[128,8]{0,1:T(8,128)}, u32[]{:S(2)}) copy-start(f32[128,8]{0,1:T(8,128)} %copy-done.43) | copy-start | bytes 12292
  640.3 135.2 %copy-start.28 = (f32[128,64]{1,0:T(8,128)S(1)}, f32[128,64]{1,0:T(8,128)}, u32[]{:S(2)}) copy-start(f32[128,64]{1,0:T(8,128)} %copy-done.27) | copy-start | bytes 98308
  640.3 135.2 %copy-start.35 = (f32[128,64]{1,0:T(8,128)S(1)}, f32[128,64]{1,0:T(8,128)}, u32[]{:S(2)}) copy-start(f32[128,64]{1,0:T(8,128)} %get-tuple-element.776) | copy-start | bytes 98308
  640.3 325.3 %all-reduce.15.cloned.1.call-start = ((), (), s32[]{:S(2)}) async-start(), calls=%async_computation.15 | async-start | bytes 2097152 | tf_op jit(solution)/shard_map/psum | solution.py:231
  781.5 67.8 %copy-start.18 = (f32[128,4,128]{2,1,0:T(4,128)S(1)}, f32[128,4,128]{2,1,0:T(4,128)}, u32[]{:S(2)}) copy-start(f32[128,4,128]{2,1,0:T(4,128)} %copy-done.17) | copy-start | bytes 786436
  854.7 71.6 %copy-start.21 = (bf16[128,1024]{1,0:T(8,128)(2,1)S(1)}, bf16[128,1024]{1,0:T(8,128)(2,1)}, u32[]{:S(2)}) copy-start(bf16[128,1024]{1,0:T(8,128)(2,1)} %copy-done.20) | copy-start | bytes 786436
  926.0 491.2 %all-reduce.13.cloned.1.call-start = ((), (), s32[]{:S(2)}) async-start(), calls=%async_computation.14 | async-start | bytes 50462720 | tf_op jit(solution)/shard_map/psum | solution.py:349
  950.7 14.9 %copy-start.51 = (f32[128]{0:T(128)S(1)}, f32[128]{0:T(128)}, u32[]{:S(2)}) copy-start(f32[128]{0:T(128)} %copy-done.48) | copy-start | bytes 1540
  950.7 16.5 %copy-start.45 = (f32[2048]{0:T(1024)S(1)}, f32[2048]{0:T(1024)}, u32[]{:S(2)}) copy-start(f32[2048]{0:T(1024)} %get-tuple-element.659) | copy-start | bytes 24580
  950.7 80.8 %copy-start.56 = (f32[128]{0:T(128)S(1)}, f32[128]{0:T(128)}, u32[]{:S(2)}) copy-start(f32[128]{0:T(128)} %copy-done.54) | copy-start | bytes 1540
  950.7 80.8 %copy-start.62 = (f32[128]{0:T(128)S(1)}, f32[128]{0:T(128)}, u32[]{:S(2)}) copy-start(f32[128]{0:T(128)} %copy-done.60) | copy-start | bytes 1540
  (63 other events, 275.1 us)
Sparse Core Ops, SparseCore 0:
  12.8 43.9 all-gather.6
  59.6 40.1 all-gather.4
  131.5 35.7 all-reduce.8
  172.9 126.8 all-gather.10
  302.6 73.0 all-gather.8
  380.2 176.7 reduce-scatter.6
  560.0 27.5 all-reduce.10
  591.8 178.5 reduce-scatter.4
  774.8 71.4 reduce-scatter.8
  851.0 71.3 reduce-scatter.10
  926.1 39.3 all-reduce.14
  972.2 444.9 all-reduce.12
